TPU v7x, 512 devices: a whole 4x4x16 slice. The times are simulated.
512 devices in a mesh: grp: 16 (over y, x), dev: 32 (over z, core).
Axes of the slice: x: 4, y: 4, z: 16, core: 2. Of those that a mesh axis runs over, the one named last changes fastest.
Arguments:
- points: float32 [3, 524288], P(None, ('grp', 'dev')), may hold values from 0 to 2
- charges: float32 [16, 524288], P(None, ('grp', 'dev')), may hold values from -6 to 6
- morton: int32 [524288], P(('grp', 'dev')), may hold values from 0 to 1023, as said below
- neighbours: int32 [2048, 8], P(('grp', 'dev')), may hold values from 0 to 2047, as said below
- counts: int32 [2048], P(('grp', 'dev')), may hold values from 1 to 8
- skel_leaf: float32 [3, 524288], P(None, ('grp', 'dev')), may hold values from 0 to 2
- skel_block: float32 [3, 131072], P(None, ('grp', 'dev')), may hold values from 0 to 2
- skel_group: float32 [3, 4096], replicated, may hold values from 0 to 2
Outputs:
- potential: float32 [16, 524288], P(None, ('grp', 'dev'))
Inputs may be any that keep to these rules, and one draw needn't show every extreme that they name: `morton`: each aligned run of 1024 entries is a permutation of 0 to 1023. `neighbours`: entry [q, k] is a leaf other than q, at most 4 leaves away from q; only slots k < counts[q] are used.
All inputs are finite; a program needn't handle non-finite values.
Results may differ from a plain program's by a relative error of at most 0.0003.
Values sent between devices are 32-bit elements; how exact they have to be, the bound alone decides.
No kernel may reach another device: no remote copies, remote signals or barrier semaphores. Data moves between devices by JAX's collectives and lax.ppermute only.
A program may use at most 64 MiB of HBM per device.

v0:
```python
import math
import jax
import jax.numpy as jnp
from jax import lax
from jax.sharding import PartitionSpec as P

width_sq = 0.1
gain_factor = 5.0


def extended_2(cells, sides, width):
    for axis, dim in sides:
        count = lax.axis_size(axis)
        ends = count - 1
        head = lax.slice_in_dim(cells, 0, width, axis=dim)
        tail = lax.slice_in_dim(cells, cells.shape[dim] - width, cells.shape[dim], axis=dim)
        cells = jnp.concatenate(
            [
                lax.ppermute(tail, axis, [(i, (i + 1) % count) for i in range(ends)]),
                cells,
                lax.ppermute(head, axis, [((i + 1) % count, i) for i in range(ends)]),
            ],
            axis=dim,
        )
    return cells


def kernel_tile(source, target):
    distance = (source[0][:, None] - target[0][None, :]) ** 2
    distance = distance + (source[1][:, None] - target[1][None, :]) ** 2
    distance = distance + (source[2][:, None] - target[2][None, :]) ** 2
    return jnp.exp(-distance / width_sq)


def translate(values, source, target, term_count):
    product = jnp.dot(
        values,
        kernel_tile(source, target),
        precision=lax.Precision.HIGHEST,
        preferred_element_type=jnp.float32,
    )
    return gain_factor / math.sqrt(term_count) * product


def far_sum(running, weights, skeleton, target, own_member, skel_rank, term_count):
    span_cols = weights.shape[1]
    block_cols = min(skel_rank, span_cols)

    def one_block(block_index, partial_value):
        column = block_index * block_cols
        piece_w = lax.dynamic_slice_in_dim(weights, column, block_cols, 1)
        piece_s = lax.dynamic_slice_in_dim(skeleton, column, block_cols, 1)
        member = column // skel_rank
        keep_mask = jnp.where(member == own_member, 0.0, 1.0)
        return partial_value + keep_mask * translate(piece_w, piece_s, target, term_count)

    return lax.fori_loop(0, span_cols // block_cols, one_block, running)


def body(points, charges, morton, neighbours, counts, skel_leaf, skel_block, skel_group):
    n_groups = lax.axis_size("grp")
    n_blocks = lax.axis_size("dev")
    vectors, block_pts = charges.shape
    leaf_count = counts.shape[0]
    leaf_size = block_pts // leaf_count
    skel_rank = skel_block.shape[1]
    slot_total = neighbours.shape[1]
    group_id = lax.axis_index("grp")
    member_id = lax.axis_index("dev")
    block_id = group_id * n_blocks + member_id
    sorted_pts = jnp.take(points, morton, axis=1)
    sorted_chg = jnp.take(charges, morton, axis=1)
    leaf_pts = sorted_pts.reshape(3, leaf_count, leaf_size).transpose(1, 0, 2)
    leaf_chg = sorted_chg.reshape(vectors, leaf_count, leaf_size).transpose(1, 0, 2)
    leaf_skel = skel_leaf.reshape(3, leaf_count, skel_rank).transpose(1, 0, 2)
    leaf_weights = lax.map(
        lambda inputs: translate(inputs[0], inputs[1], inputs[2], leaf_size),
        (leaf_chg, leaf_pts, leaf_skel),
    )
    lifted = lax.map(
        lambda inputs: translate(inputs[0], inputs[1], skel_block, leaf_count * skel_rank),
        (leaf_weights, leaf_skel),
    )
    block_weights = jnp.sum(lifted, axis=0)
    own_group = lax.dynamic_slice_in_dim(skel_group, group_id * skel_rank, skel_rank, 1)
    raised = translate(block_weights, skel_block, own_group, n_blocks * skel_rank)
    empty = jnp.zeros((vectors, skel_rank), jnp.float32)
    group_terms = (n_groups - 1) * skel_rank
    group_weights = lax.psum(raised, "dev")
    group_field = far_sum(
        empty,
        lax.all_gather(group_weights, "grp", axis=1, tiled=True),
        skel_group,
        own_group,
        group_id,
        skel_rank,
        group_terms,
    )
    peer_field = far_sum(
        empty,
        lax.all_gather(block_weights, "dev", axis=1, tiled=True),
        lax.all_gather(skel_block, "dev", axis=1, tiled=True),
        skel_block,
        member_id,
        skel_rank,
        (n_blocks - 1) * skel_rank,
    )
    block_field = peer_field + translate(group_field, own_group, skel_block, skel_rank)
    leaf_field = lax.map(
        lambda target: translate(block_field, skel_block, target, skel_rank), leaf_skel
    )
    stacked = jnp.concatenate([sorted_pts, sorted_chg], axis=0)
    extended = extended_2(stacked, ((("grp", "dev"), 1),), block_pts)
    ext_leaves = extended.reshape(3 + vectors, 3 * leaf_count, leaf_size).transpose(1, 0, 2)
    first_leaf = block_id * leaf_count - leaf_count

    def near_leaf(inputs):
        own_pts, own_chg, own_field, own_skel, row_nbr, row_count = inputs
        direct = translate(own_chg, own_pts, own_pts, leaf_size)
        direct = direct + translate(own_field, own_skel, own_pts, skel_rank)

        def one_slot(slot_index, running):
            source = lax.dynamic_index_in_dim(
                ext_leaves, row_nbr[slot_index] - first_leaf, 0, keepdims=False
            )
            tile_term = translate(source[3:], source[:3], own_pts, leaf_size)
            return running + jnp.where(slot_index < row_count, tile_term, jnp.zeros_like(tile_term))

        return lax.fori_loop(0, slot_total, one_slot, direct)

    potential = lax.map(near_leaf, (leaf_pts, leaf_chg, leaf_field, leaf_skel, neighbours, counts))
    return potential.transpose(1, 0, 2).reshape(vectors, block_pts)


def solution(mesh):
    return jax.shard_map(
        body,
        mesh=mesh,
        in_specs=(
            P(None, ("grp", "dev")),
            P(None, ("grp", "dev")),
            P(("grp", "dev")),
            P(("grp", "dev"), None),
            P(("grp", "dev")),
            P(None, ("grp", "dev")),
            P(None, ("grp", "dev")),
            P(),
        ),
        out_specs=P(None, ("grp", "dev")),
        check_vma=False,
    )
```

profile of v0, /device:TPU:8, one launch (start us, length us, event | category | flops | bytes accessed | tf_op | source)
XLA Modules:
  0.0 328.9 jit_solution(2411669421259678028)
XLA Ops:
  0.0 0.8 compare_and_fusion
  0.8 0.9 copy.25
  1.7 2.8 gather_fusion.1
  4.9 0.6 copy-done.2
  5.8 2.8 gather_fusion
  9.0 12.9 %collective-permute-start.1 = (f32[19,1024]{1,0:T(8,128)S(1)}, f32[19,1024]{1,0:T(8,128)S(1)}, u32[]{:S(2)}, u32[]{:S(2)}) collective-permute-start(f32[19,1024]{1,0:T(8,128)S(1)} %pad_maximum_fusion.1), channel_id=1, source_target_pairs={{1,0},{2,1},{3,2},{4,3},{5,4},{6,5},{7,6},{8,7},{9,8},{10,9},{11,1... | collective-permute-start | bytes 233480 | tf_op jit(solution)/shard_map/ppermute | solution.py:21
  21.9 1.9 collective-permute-start
  23.9 0.6 copy-done
  24.6 27.1 %all_gather.10 = f32[3,8192]{1,0:T(4,128)S(1)} all-gather(f32[3,256]{1,0:T(4,128)S(1)} %copy-done), channel_id=1, replica_groups=mesh['grp'=16,'dev'=32] {'dev'}, dimensions={1}, use_global_device_ids=true | all-gather | bytes 101376 | tf_op jit(solution)/shard_map/all_gather | solution.py:102
  52.1 0.7 copy-done.1
  52.8 1.6 while.85
  54.5 1.7 while.86
  56.2 30.2 %all_gather.9 = f32[16,8192]{1,0:T(8,128)S(1)} all-gather(f32[16,256]{1,0:T(8,128)S(1)} %reduce_sum.9), channel_id=1, replica_groups=mesh['grp'=16,'dev'=32] {'dev'}, dimensions={1}, use_global_device_ids=true | all-gather | bytes 540672 | tf_op jit(solution)/shard_map/all_gather | solution.py:101
  86.4 0.7 constant_dynamic-slice_fusion.25
  87.1 0.9 constant_dynamic-slice_fusion.24
  88.3 90.3 %psum.7 = f32[16,256]{1,0:T(8,128)S(1)} all-reduce(f32[16,256]{1,0:T(8,128)S(1)} %convolution_multiply_fusion.7), channel_id=1, replica_groups=mesh['grp'=16,'dev'=32] {'dev'}, use_global_device_ids=true, to_apply=%region_7.8 | all-reduce | flops 4096 | bytes 32768 | tf_op jit(solution)/shard_map/psum | solution.py:89
  178.7 24.5 %all_gather.11 = f32[16,4096]{1,0:T(8,128)S(1)} all-gather(f32[16,256]{1,0:T(8,128)S(1)} %psum.7), channel_id=1, replica_groups=mesh['grp'=16,'dev'=32] {'grp'}, dimensions={1}, use_global_device_ids=true | all-gather | bytes 278528 | tf_op jit(solution)/shard_map/all_gather | solution.py:92
  203.1 21.3 %while.91 = (s32[]{:T(128)}, f32[16,256]{1,0:T(8,128)S(1)}, f32[16,4096]{1,0:T(8,128)S(1)}, f32[3,4096]{1,0:T(4,128)}, f32[3,256]{1,0:T(4,128)S(1)}, /*index=5*/...) while((s32[]{:T(128)}, f32[16,256]{1,0:T(8,128)S(1)}, ...), condition=%wide.region_9.10_spmd.clone, body=%wide.region_8.9_spmd.clone.sunk | while | flops 13250586 | bytes 68032 | solution.py:57
  203.1 0.9 constant_dynamic-slice_fusion.38
  204.5 0.9 constant_dynamic-slice_fusion.38
  205.8 0.9 constant_dynamic-slice_fusion.38
  207.1 0.9 constant_dynamic-slice_fusion.38
  208.5 0.9 constant_dynamic-slice_fusion.38
  209.8 0.9 constant_dynamic-slice_fusion.38
  211.1 0.9 constant_dynamic-slice_fusion.38
  212.5 0.9 constant_dynamic-slice_fusion.38
  213.8 0.9 constant_dynamic-slice_fusion.38
  215.1 0.9 constant_dynamic-slice_fusion.38
  216.5 0.9 constant_dynamic-slice_fusion.38
  217.8 0.9 constant_dynamic-slice_fusion.38
  219.1 0.9 constant_dynamic-slice_fusion.38
  220.5 0.9 constant_dynamic-slice_fusion.38
  221.8 0.9 constant_dynamic-slice_fusion.38
  223.1 0.9 constant_dynamic-slice_fusion.38
  224.4 17.1 %while.90 = (s32[]{:T(128)}, f32[16,256]{1,0:T(8,128)S(1)}, f32[16,8192]{1,0:T(8,128)S(1)}, f32[3,8192]{1,0:T(4,128)S(1)}, f32[3,256]{1,0:T(4,128)S(1)}, /*index...) while((s32[]{:T(128)}, f32[16,256]{1,0:T(8,128)S(1)}, ...), condition=%wide.region_6.7_spmd.clone, body=%wide.region_5.6_spmd.clone.sunk | while | flops 13250586 | bytes 68032 | solution.py:57
  241.9 1.8 while.87
  244.0 0.6 copy-done.4
  244.7 83.6 %while.89 = (s32[]{:T(128)}, f32[4,16,256]{2,1,0:T(8,128)S(1)}, f32[4,16,256]{2,1,0:T(8,128)S(1)}, f32[4,3,256]{2,1,0:T(4,128)S(1)}, f32[4,16,256]{2,1,0:T(8,128...) while((s32[]{:T(128)}, f32[4,16,256]{2,1,0:T(8,128)S(1)}, ...), condition=%wide.region_15.16_spmd, body=%wide.region_12.15_spmd.sunk | while | flops 39735312 | bytes 213682 | solution.py:131
  245.3 0.7 fusion.275
  246.8 18.8 %while.92 = (s32[]{:T(128)}, f32[16,256]{1,0:T(8,128)S(1)}, s32[]{:T(128)}, s32[8]{0:T(128)S(1)}, s32[]{:T(128)}, /*index=5*/f32[12,19,256]{2,1,0:T(8,128)S(1)},...) while((s32[]{:T(128)}, f32[16,256]{1,0:T(8,128)S(1)}, ...), condition=%wide.region_14.14_spmd, body=%wide.region_13.13_spmd.sunk | while | flops 13250570 | bytes 67841 | solution.py:129
  247.4 0.6 dynamic_slice.147
  266.2 0.7 fusion.275
  267.6 18.8 %while.92 = (s32[]{:T(128)}, f32[16,256]{1,0:T(8,128)S(1)}, s32[]{:T(128)}, s32[8]{0:T(128)S(1)}, s32[]{:T(128)}, /*index=5*/f32[12,19,256]{2,1,0:T(8,128)S(1)},...) while((s32[]{:T(128)}, f32[16,256]{1,0:T(8,128)S(1)}, ...), condition=%wide.region_14.14_spmd, body=%wide.region_13.13_spmd.sunk | while | flops 13250570 | bytes 67841 | solution.py:129
  287.0 0.7 fusion.275
  288.5 18.8 %while.92 = (s32[]{:T(128)}, f32[16,256]{1,0:T(8,128)S(1)}, s32[]{:T(128)}, s32[8]{0:T(128)S(1)}, s32[]{:T(128)}, /*index=5*/f32[12,19,256]{2,1,0:T(8,128)S(1)},...) while((s32[]{:T(128)}, f32[16,256]{1,0:T(8,128)S(1)}, ...), condition=%wide.region_14.14_spmd, body=%wide.region_13.13_spmd.sunk | while | flops 13250570 | bytes 67841 | solution.py:129
  307.9 0.7 fusion.275
  309.4 18.8 %while.92 = (s32[]{:T(128)}, f32[16,256]{1,0:T(8,128)S(1)}, s32[]{:T(128)}, s32[8]{0:T(128)S(1)}, s32[]{:T(128)}, /*index=5*/f32[12,19,256]{2,1,0:T(8,128)S(1)},...) while((s32[]{:T(128)}, f32[16,256]{1,0:T(8,128)S(1)}, ...), condition=%wide.region_14.14_spmd, body=%wide.region_13.13_spmd.sunk | while | flops 13250570 | bytes 67841 | solution.py:129
  328.2 0.6 copy.31
  (296 shorter events, 66.9 us)
Async XLA Ops:
  0.0 0.8 copy-start.3
  4.7 0.8 copy-start.2
  9.0 234.7 %collective-permute-start.1 = (f32[19,1024]{1,0:T(8,128)S(1)}, f32[19,1024]{1,0:T(8,128)S(1)}, u32[]{:S(2)}, u32[]{:S(2)}) collective-permute-start(f32[19,1024]{1,0:T(8,128)S(1)} %pad_maximum_fusion.1), channel_id=1, source_target_pairs={{1,0},{2,1},{3,2},{4,3},{5,4},{6,5},{7,6},{8,7},{9,8},{10,9},{11,1... | collective-permute-start | bytes 233480 | tf_op jit(solution)/shard_map/ppermute | solution.py:21
  21.9 221.8 %collective-permute-start = (f32[19,1024]{1,0:T(8,128)S(1)}, f32[19,1024]{1,0:T(8,128)S(1)}, u32[]{:S(2)}, u32[]{:S(2)}) collective-permute-start(f32[19,1024]{1,0:T(8,128)S(1)} %pad_maximum_fusion.1), channel_id=1, source_target_pairs={{0,1},{1,2},{2,3},{3,4},{4,5},{5,6},{6,7},{7,8},{8,9},{9,10},{10,1... | collective-permute-start | bytes 233480 | tf_op jit(solution)/shard_map/ppermute | solution.py:19
  23.9 0.7 copy-start
  52.1 0.7 copy-start.1
  244.0 0.7 copy-start.4
where the time goes:
time: 331 us; the launch traced here: 329 us
  blocking collectives  172 us (52%)
  local copies, waits for them, and re-layouts  55.4 us (17%)
  loops' own time  45.1 us (14%)
  matrix products  39.9 us (12%)
  starting transfers between devices  14.8 us (4%)
    psum x1, blocking collectives, body(): group_weights = lax.psum(raised, 'dev')  90.3 us
    another operation x4, loops' own time, near_leaf(): return lax.fori_loop(0, slot_total, one_slot, direct)  41.7 us
    dot_general x102, matrix products, translate(): jnp.dot(values, kernel_tile(source, target), precision=lax.Precision.HIGH...  39.9 us
    all_gather x1, blocking collectives, body(): lax.all_gather(block_weights, 'dev', axis=1, tiled=True)  30.2 us
    all_gather x1, blocking collectives, body(): lax.all_gather(skel_block, 'dev', axis=1, tiled=True)  27.1 us
    all_gather x1, blocking collectives, body(): lax.all_gather(group_weights, 'grp', axis=1, tiled=True)  24.5 us
    dynamic_slice x32, local copies, waits for them, and re-layouts, one_slot(): row_nbr[slot_index] - first_leaf  19.9 us
    slice x138, local copies, waits for them, and re-layouts, kernel_tile(): distance = (source[0][:, None] - target[0][None, :]) ** 2  18.6 us
  transfers between devices with their start and end apart: 2, of which 0 were waited for; matrix products, arithmetic and copies ran while one was open for 13% of the time, Pallas kernels for 0%

commit v1 on v0

--- a/solution.py
+++ b/solution.py
@@ -6,6 +6,11 @@
 
 width_sq = 0.1
 gain_factor = 5.0
+
+
+def all_by_exchange(x, axis, dim):
+    sent = jnp.stack([x] * lax.axis_size(axis))
+    return jnp.concatenate(lax.all_to_all(sent, axis, 0, 0), axis=dim)
 
 
 def extended_2(cells, sides, width):
@@ -89,7 +94,7 @@
     group_weights = lax.psum(raised, "dev")
     group_field = far_sum(
         empty,
-        lax.all_gather(group_weights, "grp", axis=1, tiled=True),
+        all_by_exchange(group_weights, "grp", 1),
         skel_group,
         own_group,
         group_id,

time: 331 us -> 320 us (0.967)
  the two profiles are of different devices: /device:TPU:8 before, /device:TPU:1 now
where the time goes in v1:
time: 320 us; the launch traced here: 318 us
  blocking collectives  155 us (48%)
  local copies, waits for them, and re-layouts  57.2 us (18%)
  loops' own time  45 us (14%)
  matrix products  39.9 us (12%)
  starting transfers between devices  19.3 us (6%)
    psum x1, blocking collectives, body(): group_weights = lax.psum(raised, 'dev')  93.9 us
    another operation x4, loops' own time, near_leaf(): return lax.fori_loop(0, slot_total, one_slot, direct)  41.6 us
    dot_general x102, matrix products, translate(): jnp.dot(values, kernel_tile(source, target), precision=lax.Precision.HIGH...  39.9 us
    all_gather x1, blocking collectives, body(): lax.all_gather(skel_block, 'dev', axis=1, tiled=True)  30.8 us
    all_gather x1, blocking collectives, body(): lax.all_gather(block_weights, 'dev', axis=1, tiled=True)  30.1 us
    dynamic_slice x32, local copies, waits for them, and re-layouts, one_slot(): row_nbr[slot_index] - first_leaf  20.8 us
    slice x138, local copies, waits for them, and re-layouts, kernel_tile(): distance = (source[0][:, None] - target[0][None, :]) ** 2  18.7 us
    ppermute x1, starting transfers between devices, extended_2(): lax.ppermute(head, axis, [((i + 1) % count, i) for i in range(ends)])  8.78 us
  transfers between devices with their start and end apart: 3, of which 0 were waited for; matrix products, arithmetic and copies ran while one was open for 7% of the time, Pallas kernels for 0%

profile of v1, /device:TPU:1, one launch (start us, length us, event | category | flops | bytes accessed | tf_op | source)
XLA Modules:
  0.0 317.7 jit_solution(4409680423787514675)
XLA Ops:
  0.0 0.8 compare_and_fusion
  0.8 0.9 copy.25
  1.7 2.8 gather_fusion.1
  5.8 2.8 gather_fusion
  9.0 8.8 %collective-permute-start.1 = (f32[19,1024]{1,0:T(8,128)S(1)}, f32[19,1024]{1,0:T(8,128)S(1)}, u32[]{:S(2)}, u32[]{:S(2)}) collective-permute-start(f32[19,1024]{1,0:T(8,128)S(1)} %pad_maximum_fusion.1), channel_id=1, source_target_pairs={{1,0},{2,1},{3,2},{4,3},{5,4},{6,5},{7,6},{8,7},{9,8},{10,9},{11,1... | collective-permute-start | bytes 233480 | tf_op jit(solution)/shard_map/ppermute | solution.py:26
  17.8 1.9 collective-permute-start
  19.8 0.7 copy-done
  20.9 0.7 copy-done.1
  21.6 1.6 while.85
  23.2 1.7 while.86
  25.0 0.9 constant_dynamic-slice_fusion.24
  26.3 93.9 %psum.7 = f32[16,256]{1,0:T(8,128)S(1)} all-reduce(f32[16,256]{1,0:T(8,128)S(1)} %convolution_multiply_fusion.7), channel_id=1, replica_groups=mesh['grp'=16,'dev'=32] {'dev'}, use_global_device_ids=true, to_apply=%region_7.8 | all-reduce | flops 4096 | bytes 32768 | tf_op jit(solution)/shard_map/psum | solution.py:94
  120.1 0.7 stack.2
  120.8 8.6 %all-to-all-start = ((f32[16,16,256]{2,1,0:T(8,128)}), f32[16,16,256]{2,1,0:T(8,128)S(1)}, u32[]{:S(2)}, u32[]{:S(2)}) async-start(f32[16,16,256]{2,1,0:T(8,128)} %stack.2), calls=%async_computation | async-start | bytes 524288 | tf_op jit(solution)/shard_map/all_to_all | solution.py:13
  129.5 30.8 %all_gather.7 = f32[3,8192]{1,0:T(4,128)S(1)} all-gather(f32[3,256]{1,0:T(4,128)S(1)} %get-tuple-element.1439), channel_id=1, replica_groups=mesh['grp'=16,'dev'=32] {'dev'}, dimensions={1}, use_global_device_ids=true | all-gather | bytes 101376 | tf_op jit(solution)/shard_map/all_gather | solution.py:107
  160.3 30.1 %all_gather.6 = f32[16,8192]{1,0:T(8,128)S(1)} all-gather(f32[16,256]{1,0:T(8,128)S(1)} %reduce_sum.9), channel_id=1, replica_groups=mesh['grp'=16,'dev'=32] {'dev'}, dimensions={1}, use_global_device_ids=true | all-gather | bytes 540672 | tf_op jit(solution)/shard_map/all_gather | solution.py:106
  190.4 17.0 %while.90 = (s32[]{:T(128)}, f32[16,256]{1,0:T(8,128)S(1)}, f32[16,8192]{1,0:T(8,128)S(1)}, f32[3,8192]{1,0:T(4,128)S(1)}, f32[3,256]{1,0:T(4,128)S(1)}, /*index...) while((s32[]{:T(128)}, f32[16,256]{1,0:T(8,128)S(1)}, ...), condition=%wide.region_6.7_spmd.clone, body=%wide.region_5.6_spmd.clone.sunk | while | flops 13250586 | bytes 68032 | solution.py:62
  207.4 0.7 constant_dynamic-slice_fusion.25
  208.4 21.3 %while.91 = (s32[]{:T(128)}, f32[16,256]{1,0:T(8,128)S(1)}, f32[16,4096]{1,0:T(8,128)S(1)}, f32[3,4096]{1,0:T(4,128)}, f32[3,256]{1,0:T(4,128)S(1)}, /*index=5*/...) while((s32[]{:T(128)}, f32[16,256]{1,0:T(8,128)S(1)}, ...), condition=%wide.region_9.10_spmd.clone, body=%wide.region_8.9_spmd.clone.sunk | while | flops 13250586 | bytes 68032 | solution.py:62
  208.5 0.9 constant_dynamic-slice_fusion.38
  209.8 0.9 constant_dynamic-slice_fusion.38
  211.1 0.9 constant_dynamic-slice_fusion.38
  212.5 0.9 constant_dynamic-slice_fusion.38
  213.8 0.9 constant_dynamic-slice_fusion.38
  215.1 0.9 constant_dynamic-slice_fusion.38
  216.5 0.9 constant_dynamic-slice_fusion.38
  217.8 0.9 constant_dynamic-slice_fusion.38
  219.1 0.9 constant_dynamic-slice_fusion.38
  220.5 0.9 constant_dynamic-slice_fusion.38
  221.8 0.9 constant_dynamic-slice_fusion.38
  223.1 0.9 constant_dynamic-slice_fusion.38
  224.5 0.9 constant_dynamic-slice_fusion.38
  225.8 0.9 constant_dynamic-slice_fusion.38
  227.1 0.9 constant_dynamic-slice_fusion.38
  228.5 0.9 constant_dynamic-slice_fusion.38
  230.2 1.8 while.87
  232.7 84.4 %while.89 = (s32[]{:T(128)}, f32[4,16,256]{2,1,0:T(8,128)S(1)}, f32[4,16,256]{2,1,0:T(8,128)S(1)}, f32[4,3,256]{2,1,0:T(4,128)S(1)}, f32[4,16,256]{2,1,0:T(8,128...) while((s32[]{:T(128)}, f32[4,16,256]{2,1,0:T(8,128)S(1)}, ...), condition=%wide.region_15.16_spmd, body=%wide.region_12.15_spmd.sunk | while | flops 39735312 | bytes 213682 | solution.py:136
  233.3 0.7 fusion.275
  234.8 19.0 %while.92 = (s32[]{:T(128)}, f32[16,256]{1,0:T(8,128)S(1)}, s32[]{:T(128)}, s32[8]{0:T(128)S(1)}, s32[]{:T(128)}, /*index=5*/f32[12,19,256]{2,1,0:T(8,128)S(1)},...) while((s32[]{:T(128)}, f32[16,256]{1,0:T(8,128)S(1)}, ...), condition=%wide.region_14.14_spmd, body=%wide.region_13.13_spmd.sunk | while | flops 13250570 | bytes 67841 | solution.py:134
  235.4 0.7 dynamic_slice.147
  237.8 0.7 dynamic_slice.147
  240.1 0.7 dynamic_slice.147
  254.4 0.7 fusion.275
  255.9 19.0 %while.92 = (s32[]{:T(128)}, f32[16,256]{1,0:T(8,128)S(1)}, s32[]{:T(128)}, s32[8]{0:T(128)S(1)}, s32[]{:T(128)}, /*index=5*/f32[12,19,256]{2,1,0:T(8,128)S(1)},...) while((s32[]{:T(128)}, f32[16,256]{1,0:T(8,128)S(1)}, ...), condition=%wide.region_14.14_spmd, body=%wide.region_13.13_spmd.sunk | while | flops 13250570 | bytes 67841 | solution.py:134
  275.5 0.7 fusion.275
  277.0 19.0 %while.92 = (s32[]{:T(128)}, f32[16,256]{1,0:T(8,128)S(1)}, s32[]{:T(128)}, s32[8]{0:T(128)S(1)}, s32[]{:T(128)}, /*index=5*/f32[12,19,256]{2,1,0:T(8,128)S(1)},...) while((s32[]{:T(128)}, f32[16,256]{1,0:T(8,128)S(1)}, ...), condition=%wide.region_14.14_spmd, body=%wide.region_13.13_spmd.sunk | while | flops 13250570 | bytes 67841 | solution.py:134
  296.6 0.7 fusion.275
  298.1 19.0 %while.92 = (s32[]{:T(128)}, f32[16,256]{1,0:T(8,128)S(1)}, s32[]{:T(128)}, s32[8]{0:T(128)S(1)}, s32[]{:T(128)}, /*index=5*/f32[12,19,256]{2,1,0:T(8,128)S(1)},...) while((s32[]{:T(128)}, f32[16,256]{1,0:T(8,128)S(1)}, ...), condition=%wide.region_14.14_spmd, body=%wide.region_13.13_spmd.sunk | while | flops 13250570 | bytes 67841 | solution.py:134
  (299 shorter events, 68.5 us)
Async XLA Ops:
  0.0 0.8 copy-start.3
  4.8 0.8 copy-start.2
  9.0 199.1 %collective-permute-start.1 = (f32[19,1024]{1,0:T(8,128)S(1)}, f32[19,1024]{1,0:T(8,128)S(1)}, u32[]{:S(2)}, u32[]{:S(2)}) collective-permute-start(f32[19,1024]{1,0:T(8,128)S(1)} %pad_maximum_fusion.1), channel_id=1, source_target_pairs={{1,0},{2,1},{3,2},{4,3},{5,4},{6,5},{7,6},{8,7},{9,8},{10,9},{11,1... | collective-permute-start | bytes 233480 | tf_op jit(solution)/shard_map/ppermute | solution.py:26
  17.8 190.3 %collective-permute-start = (f32[19,1024]{1,0:T(8,128)S(1)}, f32[19,1024]{1,0:T(8,128)S(1)}, u32[]{:S(2)}, u32[]{:S(2)}) collective-permute-start(f32[19,1024]{1,0:T(8,128)S(1)} %pad_maximum_fusion.1), channel_id=1, source_target_pairs={{0,1},{1,2},{2,3},{3,4},{4,5},{5,6},{6,7},{7,8},{8,9},{9,10},{10,1... | collective-permute-start | bytes 233480 | tf_op jit(solution)/shard_map/ppermute | solution.py:24
  19.8 0.7 copy-start
  20.8 0.7 copy-start.1
  120.8 87.6 %all-to-all-start = ((f32[16,16,256]{2,1,0:T(8,128)}), f32[16,16,256]{2,1,0:T(8,128)S(1)}, u32[]{:S(2)}, u32[]{:S(2)}) async-start(f32[16,16,256]{2,1,0:T(8,128)} %stack.2), calls=%async_computation | async-start | bytes 524288 | tf_op jit(solution)/shard_map/all_to_all | solution.py:13
  232.0 0.7 copy-start.4
